TPU v7x, 128 devices: a whole 4x4x4 slice. The times are simulated.
128 devices in a mesh: req: 8 (over z, core), seq: 16 (over x, y).
Axes of the slice: x: 4, y: 4, z: 4, core: 2. Of those that a mesh axis runs over, the one named last changes fastest.
Arguments:
- token_ids: int32 [64, 4], replicated, may hold values from 0 to 127999, as said below
- embed_table: bfloat16 [128000, 1024], P(('req', 'seq')), may hold values from -6 to 6
- ln_gains: float32 [4, 1024], replicated, may hold values from 0.25 to 1.75
- ln_biases: float32 [4, 1024], replicated, may hold values from -1.5 to 1.5
- rel_table: bfloat16 [512, 1024], replicated, may hold values from -6 to 6
- w_qkv: bfloat16 [1024, 3072], replicated, may hold values from -0.1875 to 0.1875
- w_out: bfloat16 [1024, 1024], replicated, may hold values from -0.1875 to 0.1875
- cache_keys: bfloat16 [64, 8192, 1024], P('req', 'seq'), may hold values from -3000 to 3000
- cache_values: bfloat16 [64, 8192, 1024], P('req', 'seq'), may hold values from -6 to 6
- lengths: int32 [64], P('req'), may hold values from 129 to 8192, as said below
- window_starts: int32 [64], P('req'), may hold values from 4 to 4096, as said below
- cache_buckets: int32 [64, 4, 8192], P('req', None, 'seq'), may hold values from 0 to 511
- new_buckets: int32 [64, 4, 4], P('req'), may hold values from 0 to 511
- w_in: bfloat16 [4096, 1024], P('seq'), may hold values from -0.1875 to 0.1875
- w_down: bfloat16 [4096, 1024], P('seq'), may hold values from -0.09375 to 0.09375
Outputs:
- layer_out: bfloat16 [64, 4, 1024], P('req')
Inputs may be any that keep to these rules, and one draw needn't show every extreme that they name: `token_ids`: every aligned block of 1000 ids holds the id of at least one new token. `lengths`: some request has length 8192. window_starts = max(4, lengths - 4096) for each request.
All inputs are finite; a program needn't handle non-finite values.
Results may differ from a plain program's by a relative error of at most 0.018.
Values may be sent and summed in bfloat16 or wider, within the bound.
A program may use at most 192 MiB of HBM per device.

v0:
```python
import math
import jax
import jax.numpy as jnp
from jax import lax
from jax.sharding import PartitionSpec as P

HEADS = 16
HEAD_DIM = 64
SINKS = 4
norm_epsilon = 1e-06
masked_score = -1e30


def layer_norm(values, gain, shift):
    center = values - jnp.mean(values, axis=-1, keepdims=True)
    spread = jnp.mean(center * center, axis=-1, keepdims=True)
    return center * lax.rsqrt(spread + norm_epsilon) * gain + shift


def expand_rows(rows_x, in_rows, down_rows):
    inner = lax.dot_general(
        rows_x, in_rows, (((1,), (1,)), ((), ())), preferred_element_type=jnp.float32
    )
    inner = jax.nn.gelu(inner, approximate=False).astype(jnp.bfloat16)
    return jnp.dot(inner, down_rows, preferred_element_type=jnp.float32)


def shards(
    token_ids,
    embed_table,
    ln_gains,
    ln_biases,
    rel_table,
    w_qkv,
    w_out,
    cache_keys,
    cache_values,
    lengths,
    window_starts,
    cache_buckets,
    new_buckets,
    w_in,
    w_down,
):
    group_reqs, piece_len, width = cache_keys.shape
    new_count = token_ids.shape[1]
    vocab_rows = embed_table.shape[0]
    bucket_count = rel_table.shape[0]
    group_rows = group_reqs * new_count
    seq_index = lax.axis_index("seq")
    req_index = lax.axis_index("req")
    owner_index = req_index * lax.axis_size("seq") + seq_index
    local_ids = token_ids.reshape(-1) - owner_index * vocab_rows
    one_hot = (local_ids[:, None] == jnp.arange(vocab_rows, dtype=jnp.int32)[None, :]).astype(
        jnp.bfloat16
    )
    looked_up = jnp.dot(one_hot, embed_table, preferred_element_type=jnp.float32)
    summed = lax.psum(looked_up, ("req", "seq"))
    own_rows = lax.dynamic_slice_in_dim(summed, req_index * group_rows, group_rows, 0)
    hidden_zero = layer_norm(own_rows, ln_gains[0], ln_biases[0]).astype(jnp.bfloat16)
    relative = layer_norm(rel_table.astype(jnp.float32), ln_gains[3], ln_biases[3]).astype(
        jnp.bfloat16
    )
    pos_query = jnp.dot(relative, w_qkv[:, :width], preferred_element_type=jnp.float32).astype(
        jnp.bfloat16
    )
    pos_key = jnp.dot(
        relative, w_qkv[:, width : 2 * width], preferred_element_type=jnp.float32
    ).astype(jnp.bfloat16)
    projected = jnp.dot(hidden_zero, w_qkv, preferred_element_type=jnp.float32).astype(jnp.bfloat16)
    queries = projected[:, :width].reshape(group_reqs, new_count, HEADS, HEAD_DIM)
    fresh_keys = projected[:, width : 2 * width].reshape(group_reqs, new_count, HEADS, HEAD_DIM)
    fresh_values = projected[:, 2 * width :].reshape(group_reqs, new_count, HEADS, HEAD_DIM)
    pos_key_heads = pos_key.reshape(bucket_count, HEADS, HEAD_DIM)
    reversed_query_heads = pos_query[::-1].reshape(bucket_count, HEADS, HEAD_DIM)
    query_table = jnp.einsum(
        "rthd,bhd->rhtb", queries, pos_key_heads, preferred_element_type=jnp.float32
    )
    score_scale = 1.0 / math.sqrt(3 * HEAD_DIM)
    bucket_range = jnp.arange(bucket_count, dtype=jnp.int32)
    first_place = seq_index * piece_len
    positions = first_place + jnp.arange(piece_len, dtype=jnp.int32)
    piece_live = (first_place < lengths) & (
        (first_place < SINKS) | (first_place + piece_len > window_starts)
    )
    key_heads = cache_keys.reshape(group_reqs, piece_len, HEADS, HEAD_DIM)
    value_heads = cache_values.reshape(group_reqs, piece_len, HEADS, HEAD_DIM)

    def piece_scores(queries_one, table_one, keys_one, buckets_one, length_one, start_one):
        content = jnp.einsum(
            "thd,phd->htp", queries_one, keys_one, preferred_element_type=jnp.float32
        )
        selector = (buckets_one[:, :, None] == bucket_range[None, None, :]).astype(jnp.float32)
        to_pos = jnp.einsum("tpb,htb->htp", selector, table_one, precision=lax.Precision.HIGHEST)
        key_table = jnp.einsum(
            "phd,bhd->hpb", keys_one, reversed_query_heads, preferred_element_type=jnp.float32
        )
        from_pos = jnp.einsum("tpb,hpb->htp", selector, key_table, precision=lax.Precision.HIGHEST)
        allowed = (positions < length_one) & ((positions < SINKS) | (positions >= start_one))
        return jnp.where(
            allowed[None, None, :], (content + to_pos + from_pos) * score_scale, masked_score
        )

    def score_step(items):
        queries_one, table_one, keys_one, buckets_one, length_one, start_one, live_one = items
        return piece_scores(queries_one, table_one, keys_one, buckets_one, length_one, start_one)

    scores = lax.map(
        score_step,
        (queries, query_table, key_heads, cache_buckets, lengths, window_starts, piece_live),
    )
    content_new = jnp.einsum(
        "rthd,ruhd->rhtu", queries, fresh_keys, preferred_element_type=jnp.float32
    )
    to_pos_new = jnp.take_along_axis(
        query_table,
        jnp.broadcast_to(new_buckets[:, None], (group_reqs, HEADS, new_count, new_count)),
        axis=3,
    )
    gathered_new = jnp.take(pos_query, bucket_count - 1 - new_buckets, axis=0).reshape(
        group_reqs, new_count, new_count, HEADS, HEAD_DIM
    )
    from_pos_new = jnp.einsum(
        "rtuhd,ruhd->rhtu", gathered_new, fresh_keys, preferred_element_type=jnp.float32
    )
    causal = jnp.arange(new_count)[None, :] <= jnp.arange(new_count)[:, None]
    fresh_scores = jnp.where(
        causal, (content_new + to_pos_new + from_pos_new) * score_scale, masked_score
    )
    row_max = jnp.maximum(lax.pmax(jnp.max(scores, axis=-1), "seq"), jnp.max(fresh_scores, axis=-1))

    def weigh_piece(scores_one, max_one, values_one):
        exp_terms = jnp.exp(scores_one - max_one[:, :, None])
        numerator = jnp.einsum(
            "htp,phd->thd",
            exp_terms.astype(jnp.bfloat16),
            values_one,
            preferred_element_type=jnp.float32,
        )
        return (numerator, jnp.sum(exp_terms, axis=-1))

    def weigh_step(items):
        scores_one, max_one, values_one, live_one = items
        return weigh_piece(scores_one, max_one, values_one)

    numerators, denominators = lax.map(weigh_step, (scores, row_max, value_heads, piece_live))
    numer_total, denom_total = lax.psum((numerators, denominators), "seq")
    fresh_exp = jnp.exp(fresh_scores - row_max[..., None])
    fresh_numer = jnp.einsum(
        "rhtu,ruhd->rthd",
        fresh_exp.astype(jnp.bfloat16),
        fresh_values,
        preferred_element_type=jnp.float32,
    )
    denom_all = jnp.transpose(denom_total + jnp.sum(fresh_exp, axis=-1), (0, 2, 1))
    attended = (
        ((numer_total + fresh_numer) / denom_all[..., None])
        .astype(jnp.bfloat16)
        .reshape(group_rows, width)
    )
    attn_out = jnp.dot(attended, w_out, preferred_element_type=jnp.float32)
    hidden_one = layer_norm(
        hidden_zero.astype(jnp.float32) + attn_out, ln_gains[1], ln_biases[1]
    ).astype(jnp.bfloat16)
    partial_mlp = expand_rows(hidden_one, w_in, w_down)
    mlp_out = lax.psum(partial_mlp.astype(jnp.bfloat16), "seq").astype(jnp.float32)
    layer_out = layer_norm(
        hidden_one.astype(jnp.float32) + mlp_out, ln_gains[2], ln_biases[2]
    ).astype(jnp.bfloat16)
    return layer_out.reshape(group_reqs, new_count, width)


def solution(mesh):
    in_specs = (
        P(),
        P(("req", "seq"), None),
        P(),
        P(),
        P(),
        P(),
        P(),
        P("req", "seq", None),
        P("req", "seq", None),
        P("req"),
        P("req"),
        P("req", None, "seq"),
        P("req", None, None),
        P("seq", None),
        P("seq", None),
    )
    out_specs = P("req", None, None)
    return jax.shard_map(shards, mesh=mesh, in_specs=in_specs, out_specs=out_specs, check_vma=False)
```

profile of v0, /device:TPU:0, one launch (start us, length us, event | category | flops | bytes accessed | tf_op | source)
XLA Modules:
  0.0 749.9 jit_solution(12523177118049195866)
XLA Ops:
  7.6 3.4 fusion.55
  13.0 2.9 fusion.49
  16.0 3.9 fusion.46
  20.9 10.3 %rev.3 = bf16[512,1024]{1,0:T(8,128)(2,1)} reverse(bf16[512,1024]{1,0:T(8,128)(2,1)S(1)} %fusion.49), dimensions={0} | reverse | bytes 2097152 | tf_op jit(solution)/shard_map/rev | solution.py:75
  32.1 2.3 copy.113
  34.7 2.3 copy.111
  37.0 11.4 %copy.110 = bf16[8,512,1024]{1,2,0:T(8,128)(2,1)} copy(bf16[8,512,1024]{2,1,0:T(8,128)(2,1)} %param.26) | data formatting | bytes 16777216 | tf_op args[7]
  48.5 11.4 %copy.109 = bf16[8,512,1024]{1,2,0:T(8,128)(2,1)} copy(bf16[8,512,1024]{2,1,0:T(8,128)(2,1)} %param.27) | data formatting | bytes 16777216 | tf_op args[8]
  60.6 100.8 %all-reduce.4.cloned.1.call-done = f32[256,1024]{1,0:T(8,128)} async-done(((f32[256,1024]{1,0:T(8,128)}), f32[256,1024]{1,0:T(8,128)}) %all-reduce.4.cloned.1.call-update) | async-done | bytes 1048592 | tf_op jit(solution)/shard_map/psum | solution.py:58
  163.6 4.1 convolution_convert_fusion
  172.7 19.5 %gather_fusion.1 = f32[2048]{0:T(1024)S(1)} fusion(f32[8,16,4,512]{3,0,2,1:T(8,128)S(1)} %convolution_bitcast_fusion.1, s32[2048]{0:T(1024)S(1)} %reshape.131), kind=kCustom, calls=%fused_computation.1 | custom fusion | bytes 49152 | tf_op jit(solution)/shard_map/jit(take_along_axis)/gather | solution.py:115
  195.7 272.9 %while.24 = (s32[]{:T(128)}, f32[8,16,4,512]{3,2,1,0:T(4,128)}, s32[8]{0:T(128)}, s32[8]{0:T(128)}, bf16[8,4,16,64]{3,1,2,0:T(4,128)(2,1)}, /*index=5*/bf16[8,51...) while((s32[]{:T(128)}, f32[8,16,4,512]{3,2,1,0:T(4,128)}, ...), condition=%wide.region_6.7_spmd.clone, body=%wide.region_5.6_spmd.clone.sunk | while | flops 945949696 | bytes 44370624 | solution.py:108
  201.1 1.6 iota_compare_fusion.8
  202.8 2.6 fusion.190
  205.4 3.6 fusion.188
  209.0 17.1 %fusion.189 = f32[512,16,4]{1,2,0:T(4,128)} fusion(f32[16,512,512]{2,1,0:T(8,128)S(1)} %fusion.188, s32[4,512]{0,1:T(8,128)S(1)} %bitcast.130), kind=kOutput, calls=%fused_computation.16.clone.1 | convolution fusion | flops 202375168 | bytes 16916480 | tf_op jit(solution)/shard_map/while/body/eval_jaxpr/tpb,hpb->htp/dot_general | solution.py:98
  227.7 2.1 fusion.192
  235.3 1.6 iota_compare_fusion.8
  236.9 2.6 fusion.190
  239.5 3.6 fusion.188
  243.1 17.1 %fusion.189 = f32[512,16,4]{1,2,0:T(4,128)} fusion(f32[16,512,512]{2,1,0:T(8,128)S(1)} %fusion.188, s32[4,512]{0,1:T(8,128)S(1)} %bitcast.130), kind=kOutput, calls=%fused_computation.16.clone.1 | convolution fusion | flops 202375168 | bytes 16916480 | tf_op jit(solution)/shard_map/while/body/eval_jaxpr/tpb,hpb->htp/dot_general | solution.py:98
  261.8 2.2 fusion.192
  269.4 1.6 iota_compare_fusion.8
  271.0 2.6 fusion.190
  273.6 3.6 fusion.188
  277.3 17.1 %fusion.189 = f32[512,16,4]{1,2,0:T(4,128)} fusion(f32[16,512,512]{2,1,0:T(8,128)S(1)} %fusion.188, s32[4,512]{0,1:T(8,128)S(1)} %bitcast.130), kind=kOutput, calls=%fused_computation.16.clone.1 | convolution fusion | flops 202375168 | bytes 16916480 | tf_op jit(solution)/shard_map/while/body/eval_jaxpr/tpb,hpb->htp/dot_general | solution.py:98
  295.9 2.1 fusion.192
  303.5 1.6 iota_compare_fusion.8
  305.1 2.6 fusion.190
  307.8 3.6 fusion.188
  311.4 17.1 %fusion.189 = f32[512,16,4]{1,2,0:T(4,128)} fusion(f32[16,512,512]{2,1,0:T(8,128)S(1)} %fusion.188, s32[4,512]{0,1:T(8,128)S(1)} %bitcast.130), kind=kOutput, calls=%fused_computation.16.clone.1 | convolution fusion | flops 202375168 | bytes 16916480 | tf_op jit(solution)/shard_map/while/body/eval_jaxpr/tpb,hpb->htp/dot_general | solution.py:98
  330.0 2.2 fusion.192
  337.6 1.6 iota_compare_fusion.8
  339.2 2.6 fusion.190
  341.9 3.6 fusion.188
  345.5 17.1 %fusion.189 = f32[512,16,4]{1,2,0:T(4,128)} fusion(f32[16,512,512]{2,1,0:T(8,128)S(1)} %fusion.188, s32[4,512]{0,1:T(8,128)S(1)} %bitcast.130), kind=kOutput, calls=%fused_computation.16.clone.1 | convolution fusion | flops 202375168 | bytes 16916480 | tf_op jit(solution)/shard_map/while/body/eval_jaxpr/tpb,hpb->htp/dot_general | solution.py:98
  364.2 2.1 fusion.192
  371.7 1.6 iota_compare_fusion.8
  373.4 2.6 fusion.190
  376.0 3.6 fusion.188
  379.6 17.1 %fusion.189 = f32[512,16,4]{1,2,0:T(4,128)} fusion(f32[16,512,512]{2,1,0:T(8,128)S(1)} %fusion.188, s32[4,512]{0,1:T(8,128)S(1)} %bitcast.130), kind=kOutput, calls=%fused_computation.16.clone.1 | convolution fusion | flops 202375168 | bytes 16916480 | tf_op jit(solution)/shard_map/while/body/eval_jaxpr/tpb,hpb->htp/dot_general | solution.py:98
  398.3 2.2 fusion.192
  407.5 2.6 fusion.190
  410.1 3.6 fusion.188
  413.7 17.1 %fusion.189 = f32[512,16,4]{1,2,0:T(4,128)} fusion(f32[16,512,512]{2,1,0:T(8,128)S(1)} %fusion.188, s32[4,512]{0,1:T(8,128)S(1)} %bitcast.130), kind=kOutput, calls=%fused_computation.16.clone.1 | convolution fusion | flops 202375168 | bytes 16916480 | tf_op jit(solution)/shard_map/while/body/eval_jaxpr/tpb,hpb->htp/dot_general | solution.py:98
  432.4 2.2 fusion.192
  441.6 2.6 fusion.190
  444.2 3.6 fusion.188
  447.8 17.1 %fusion.189 = f32[512,16,4]{1,2,0:T(4,128)} fusion(f32[16,512,512]{2,1,0:T(8,128)S(1)} %fusion.188, s32[4,512]{0,1:T(8,128)S(1)} %bitcast.130), kind=kOutput, calls=%fused_computation.16.clone.1 | convolution fusion | flops 202375168 | bytes 16916480 | tf_op jit(solution)/shard_map/while/body/eval_jaxpr/tpb,hpb->htp/dot_general | solution.py:98
  466.5 2.2 fusion.192
  470.1 73.2 %pmax.7 = f32[8,16,4]{2,1,0:T(8,128)S(1)} all-reduce(f32[8,16,4]{2,1,0:T(8,128)S(1)} %reduce_max.18), channel_id=1, replica_groups=mesh['req'=8,'seq'=16] {'seq'}, use_global_device_ids=true, to_apply=%region_8.9 | all-reduce | flops 512 | bytes 4096 | tf_op jit(solution)/shard_map/pmax | solution.py:130
  546.8 28.4 %while.23 = (s32[]{:T(128)}, f32[8,4,16,64]{3,1,2,0:T(4,128)}, f32[8,16,4]{1,2,0:T(4,128)S(1)}, bf16[8,512,16,64]{1,3,2,0:T(8,128)(2,1)}, f32[8,16,4,512]{3,2,1,0:T(4,128)}, /*index=5*/f32[8,16,4]{1,2,0:T(4,128)S(1)}, s32[]{:T(128)}) while((s32[]{:T(128)}, f32[8,4,16,64]{3,1,2,0:T(4,128)}, f32[8,16,4]{1,2,0:T(4,128)S(1)}, ...), condition=%wide.region_12.13_spmd, body=%wide.region_10.12_spmd.sunk | while | flops 4325314 | bytes 1351521 | solution.py:146
  548.1 2.3 fusion.180
  551.6 2.3 fusion.180
  555.2 2.3 fusion.180
  558.7 2.3 fusion.180
  562.3 2.3 fusion.180
  565.8 2.3 fusion.180
  569.4 2.3 fusion.180
  572.9 2.3 fusion.180
  575.4 69.6 %psum.30 = f32[8,16,4]{2,1,0:T(8,128)S(1)} all-reduce(f32[8,16,4]{2,1,0:T(8,128)S(1)} %copy.129), channel_id=1, replica_groups=mesh['req'=8,'seq'=16] {'seq'}, use_global_device_ids=true, to_apply=%region_14.15 | all-reduce | flops 512 | bytes 4096 | tf_op jit(solution)/shard_map/psum | solution.py:147
  645.0 8.7 %all-reduce.6.cloned.1.call-done = f32[8,4,16,64]{3,1,2,0:T(4,128)} async-done(((f32[8,4,16,64]{3,1,2,0:T(4,128)}), f32[8,4,16,64]{3,1,2,0:T(4,128)}) %all-reduce.6.cloned.1.call-update) | async-done | bytes 131088 | tf_op jit(solution)/shard_map/psum | solution.py:147
  657.0 2.3 convolution_convert_fusion.1
  659.3 80.3 %all-reduce.8.cloned.1.call-done = bf16[32,1024]{1,0:T(8,128)(2,1)} async-done(((bf16[32,1024]{1,0:T(8,128)(2,1)}), bf16[32,1024]{1,0:T(8,128)(2,1)}) %all-reduce.8.cloned.1.call-update) | async-done | bytes 65552 | tf_op jit(solution)/shard_map/psum | solution.py:166
  (230 shorter events, 97.2 us)
Async XLA Ops:
  6.5 648.7 %copy-start = (bf16[1024,1024]{1,0:T(8,128)(2,1)S(1)}, bf16[1024,1024]{1,0:T(8,128)(2,1)}, u32[]{:S(2)}) copy-start(bf16[1024,1024]{1,0:T(8,128)(2,1)} %param.25) | copy-start | bytes 6291460
  6.5 154.9 %all-reduce.4.cloned.1.call-start = ((), (), s32[]{:S(2)}) async-start(), calls=%async_computation | async-start | bytes 2097152 | tf_op jit(solution)/shard_map/psum | solution.py:58
  7.6 3.5 copy-start.4
  7.6 3.6 copy-start.2
  11.0 0.8 copy-start.16
  11.0 1.4 copy-start.17
  11.0 642.7 %all-reduce.6.cloned.1.call-start = ((), (), s32[]{:S(2)}) async-start(), calls=%async_computation.1 | async-start | bytes 524288 | tf_op jit(solution)/shard_map/psum | solution.py:147
  11.1 2.0 copy-start.3
  11.1 8.8 %copy-start.12 = (pred[8,4,4]{0,2,1:T(4,128)(4,1)}, pred[8,4,4]{0,2,1:T(4,128)(4,1)S(1)}, u32[]{:S(2)}) copy-start(pred[8,4,4]{0,2,1:T(4,128)(4,1)S(1)} %get-tuple-element.221) | copy-start | bytes 388
  11.2 8.7 %copy-start.5 = (s32[8,4,4]{0,2,1:T(4,128)}, s32[8,4,4]{0,2,1:T(4,128)S(1)}, u32[]{:S(2)}) copy-start(s32[8,4,4]{0,2,1:T(4,128)S(1)} %get-tuple-element.223) | copy-start | bytes 1540
  12.4 151.1 %copy-start.8 = (f32[1,1024]{1,0:T(1,128)}, f32[1,1024]{1,0:T(1,128)S(1)}, u32[]{:S(2)}) copy-start(f32[1,1024]{1,0:T(1,128)S(1)} %get-tuple-element.215) | copy-start | bytes 12292
  13.0 150.5 %copy-start.10 = (f32[1,1024]{1,0:T(1,128)}, f32[1,1024]{1,0:T(1,128)S(1)}, u32[]{:S(2)}) copy-start(f32[1,1024]{1,0:T(1,128)S(1)} %get-tuple-element.219) | copy-start | bytes 12292
  162.4 5.3 copy-start.18
  163.6 4.2 copy-start.20
  201.1 4.3 copy-start.1
  235.2 4.3 copy-start.1
  269.4 4.3 copy-start.1
  303.5 4.3 copy-start.1
  337.6 4.3 copy-start.1
  371.7 4.3 copy-start.1
  405.8 4.3 copy-start.1
  440.0 4.3 copy-start.1
  468.7 78.1 %copy-start.15 = (f32[8,16,4]{1,2,0:T(4,128)S(1)}, f32[8,16,4]{1,2,0:T(4,128)}, u32[]{:S(2)}) copy-start(f32[8,16,4]{1,2,0:T(4,128)} %custom-call.5) | copy-start | bytes 6148
  575.2 80.0 %copy-start.9 = (f32[1,1024]{1,0:T(1,128)S(1)}, f32[1,1024]{1,0:T(1,128)}, u32[]{:S(2)}) copy-start(f32[1,1024]{1,0:T(1,128)} %copy-done.8) | copy-start | bytes 12292
  575.2 80.0 %copy-start.11 = (f32[1,1024]{1,0:T(1,128)S(1)}, f32[1,1024]{1,0:T(1,128)}, u32[]{:S(2)}) copy-start(f32[1,1024]{1,0:T(1,128)} %copy-done.10) | copy-start | bytes 12292
  575.2 80.0 %copy-start.19 = (f32[32]{0:T(128)S(1)}, f32[32]{0:T(128)}, u32[]{:S(2)}) copy-start(f32[32]{0:T(128)} %copy-done.18) | copy-start | bytes 388
  575.2 80.0 %copy-start.21 = (f32[32]{0:T(128)S(1)}, f32[32]{0:T(128)}, u32[]{:S(2)}) copy-start(f32[32]{0:T(128)} %copy-done.20) | copy-start | bytes 388
  575.2 164.4 %all-reduce.8.cloned.1.call-start = ((), (), s32[]{:S(2)}) async-start(), calls=%async_computation.2 | async-start | bytes 131072 | tf_op jit(solution)/shard_map/psum | solution.py:166
  655.0 2.0 copy-start.6
  655.0 2.0 copy-start.7
  655.0 2.0 copy-start.22
  655.2 86.5 %copy-start.13 = (f32[1,1024]{1,0:T(1,128)S(1)}, f32[1,1024]{1,0:T(1,128)}, u32[]{:S(2)}) copy-start(f32[1,1024]{1,0:T(1,128)} %get-tuple-element.213) | copy-start | bytes 12292
  655.3 86.5 %copy-start.14 = (f32[1,1024]{1,0:T(1,128)S(1)}, f32[1,1024]{1,0:T(1,128)}, u32[]{:S(2)}) copy-start(f32[1,1024]{1,0:T(1,128)} %get-tuple-element.217) | copy-start | bytes 12292
Sparse Core Ops, SparseCore 0:
  12.2 149.2 all-reduce.3
  575.4 78.3 all-reduce.5
  659.4 80.1 all-reduce.7
where the time goes:
time: 753 us; the launch traced here: 750 us
  matrix products  244 us (32%)
  waiting for transfers between devices  190 us (25%)
  blocking collectives  143 us (19%)
  local copies, waits for them, and re-layouts  115 us (15%)
  other arithmetic  44.1 us (6%)
  between operations  13.6 us (2%)
    dot_general x8, matrix products, piece_scores(): jnp.einsum('tpb,hpb->htp', selector, key_table, precision=lax.Precision.H...  137 us
    psum x1, waiting for transfers between devices, shards(): summed = lax.psum(looked_up, ('req', 'seq'))  101 us
    psum x1, waiting for transfers between devices, shards(): lax.psum(partial_mlp.astype(jnp.bfloat16), 'seq').astype(jnp.float32)  80.3 us
    pmax x1, blocking collectives, shards(): lax.pmax(jnp.max(scores, axis=-1), 'seq')  73.2 us
    psum x1, blocking collectives, shards(): numer_total, denom_total = lax.psum((numerators, denominators), 'seq')  69.6 us
    dynamic_slice x40, local copies, waits for them, and re-layouts, shards(): lax.map(score_step, (queries, query_table, key_heads, cache_buckets, leng...  33.2 us
    dot_general x8, matrix products, piece_scores(): jnp.einsum('phd,bhd->hpb', keys_one, reversed_query_heads, preferred_elem...  28.9 us
    unnamed x49, local copies, waits for them, and re-layouts  24.5 us
  transfers between devices with their start and end apart: 3, of which 3 were waited for; matrix products, arithmetic and copies ran while one was open for 7% of the time, Pallas kernels for 0%

commit v1 on v0

--- a/solution.py
+++ b/solution.py
@@ -55,7 +55,7 @@
         jnp.bfloat16
     )
     looked_up = jnp.dot(one_hot, embed_table, preferred_element_type=jnp.float32)
-    summed = lax.psum(looked_up, ("req", "seq"))
+    summed = jnp.sum(lax.all_gather(looked_up, ("req", "seq")), axis=0)
     own_rows = lax.dynamic_slice_in_dim(summed, req_index * group_rows, group_rows, 0)
     hidden_zero = layer_norm(own_rows, ln_gains[0], ln_biases[0]).astype(jnp.bfloat16)
     relative = layer_norm(rel_table.astype(jnp.float32), ln_gains[3], ln_biases[3]).astype(

time: 753 us -> 1080 us (1.43)
  waiting for transfers between devices: 190 us -> 393 us
  matrix products: 244 us -> 346 us
  other arithmetic: 44.1 us -> 83.9 us
  local copies, waits for them, and re-layouts: 115 us -> 100 us
    all_gather x0 -> x1, waiting for transfers between devices: none -> 235 us  [shards(): summed = jnp.sum(lax.all_gather(looked_up, ('req', 'seq')), axis=0)]
    psum x1 -> x0, waiting for transfers between devices: 101 us -> none  [shards(): summed = lax.psum(looked_up, ('req', 'seq'))]
    psum x1, waiting for transfers between devices: 8.71 us -> 77.9 us  [shards(): numer_total, denom_total = lax.psum((numerators, denominators), 'seq')]
    dot_general x8, matrix products: 137 us -> 197 us  [piece_scores(): jnp.einsum('tpb,hpb->htp', selector, key_table, precision=lax.Precision.H...]
    dot_general x8, matrix products: 28.9 us -> 77.1 us  [piece_scores(): jnp.einsum('phd,bhd->hpb', keys_one, reversed_query_heads, preferred_elem...]
    reduce_sum x0 -> x1, other arithmetic: none -> 40.6 us  [shards(): summed = jnp.sum(lax.all_gather(looked_up, ('req', 'seq')), axis=0)]
    dynamic_slice x40, local copies, waits for them, and re-layouts: 33.2 us -> 17.6 us  [shards(): lax.map(score_step, (queries, query_table, key_heads, cache_buckets, leng...]
    unnamed x49 -> x51, local copies, waits for them, and re-layouts: 24.5 us -> 25.8 us
  transfers between devices with their start and end apart: 3 -> 3, of which waited for: 3 -> 3; matrix products, arithmetic and copies ran while one was open for 7% -> 5% of each run, Pallas kernels for 0% -> 0%
where the time goes in v1:
time: 1080 us
  waiting for transfers between devices  393 us (36%)
  matrix products  346 us (32%)
  blocking collectives  144 us (13%)
  local copies, waits for them, and re-layouts  100 us (9%)
  other arithmetic  83.9 us (8%)
  between operations  13.5 us (1%)
    all_gather x1, waiting for transfers between devices, shards(): summed = jnp.sum(lax.all_gather(looked_up, ('req', 'seq')), axis=0)  235 us
    dot_general x8, matrix products, piece_scores(): jnp.einsum('tpb,hpb->htp', selector, key_table, precision=lax.Precision.H...  197 us
    psum x1, waiting for transfers between devices, shards(): lax.psum(partial_mlp.astype(jnp.bfloat16), 'seq').astype(jnp.float32)  80.3 us
    psum x1, waiting for transfers between devices, shards(): numer_total, denom_total = lax.psum((numerators, denominators), 'seq')  77.9 us
    dot_general x8, matrix products, piece_scores(): jnp.einsum('phd,bhd->hpb', keys_one, reversed_query_heads, preferred_elem...  77.1 us
    pmax x1, blocking collectives, shards(): lax.pmax(jnp.max(scores, axis=-1), 'seq')  74.3 us
    psum x1, blocking collectives, shards(): numer_total, denom_total = lax.psum((numerators, denominators), 'seq')  69.6 us
    reduce_sum x1, other arithmetic, shards(): summed = jnp.sum(lax.all_gather(looked_up, ('req', 'seq')), axis=0)  40.6 us
  transfers between devices with their start and end apart: 3, of which 3 were waited for; matrix products, arithmetic and copies ran while one was open for 5% of the time, Pallas kernels for 0%

profile of v1, /device:TPU:0, one launch (start us, length us, event | category | flops | bytes accessed | tf_op | source)
XLA Modules:
  0.0 1081.1 jit_solution(12963132022805794936)
XLA Ops:
  7.6 3.4 fusion.55
  13.0 3.9 fusion.46
  16.9 2.3 copy.111
  20.7 3.2 fusion.49
  23.9 10.3 rev.3
  35.5 2.3 copy.113
  37.8 11.4 %copy.110 = bf16[8,512,1024]{1,2,0:T(8,128)(2,1)} copy(bf16[8,512,1024]{2,1,0:T(8,128)(2,1)} %param.26) | data formatting | bytes 16777216 | tf_op args[7]
  49.3 11.6 %copy.109 = bf16[8,512,1024]{1,2,0:T(8,128)(2,1)} copy(bf16[8,512,1024]{2,1,0:T(8,128)(2,1)} %param.27) | data formatting | bytes 16777216 | tf_op args[8]
  62.4 234.6 %all-gather.3.cloned.1.call-done = f32[32768,1024]{1,0:T(8,128)} async-done(((f32[256,1024]{1,0:T(8,128)}), f32[32768,1024]{1,0:T(8,128)}) %all-gather.3.cloned.1.call-update) | async-done | bytes 134217744 | tf_op jit(solution)/shard_map/all_gather | solution.py:58
  297.1 40.6 %reduce_sum.99 = f32[256,1024]{1,0:T(8,128)S(1)} reduce(f32[128,256,1024]{2,1,0:T(8,128)} %bitcast.6, f32[]{:T(128)} %constant.73.clone.1), dimensions={0}, to_apply=%region_0.0 | reduce | flops 33292288 | bytes 135266304 | tf_op jit(solution)/shard_map/reduce_sum | solution.py:58
  338.5 4.0 convolution_convert_fusion
  347.1 19.5 %gather_fusion.1 = f32[2048]{0:T(1024)S(1)} fusion(f32[8,16,4,512]{3,0,2,1:T(8,128)S(1)} %convolution_bitcast_fusion.1, s32[2048]{0:T(1024)S(1)} %reshape.131), kind=kCustom, calls=%fused_computation.1 | custom fusion | bytes 49152 | tf_op jit(solution)/shard_map/jit(take_along_axis)/gather | solution.py:115
  367.2 1.8 fusion.57
  369.9 1.6 fusion.145
  372.3 358.2 %while.24 = (s32[]{:T(128)}, f32[8,16,4,512]{3,2,1,0:T(4,128)}, s32[8]{0:T(128)}, s32[8]{0:T(128)}, bf16[8,4,16,64]{3,1,2,0:T(4,128)(2,1)}, /*index=5*/bf16[8,51...) while((s32[]{:T(128)}, f32[8,16,4,512]{3,2,1,0:T(4,128)}, ...), condition=%wide.region_6.7_spmd.clone, body=%wide.region_5.6_spmd.clone.sunk | while | flops 945949696 | bytes 40177104 | solution.py:108
  372.3 9.6 fusion.188
  382.8 24.6 %fusion.189 = f32[512,16,4]{1,2,0:T(4,128)} fusion(f32[16,512,512]{2,1,0:T(8,128)} %fusion.188, s32[4,512]{0,1:T(8,128)S(1)} %bitcast.130), kind=kOutput, calls=%fused_computation.16.clone.1 | convolution fusion | flops 202375168 | bytes 16916480 | tf_op jit(solution)/shard_map/while/body/eval_jaxpr/tpb,hpb->htp/dot_general | solution.py:98
  408.9 1.6 iota_compare_fusion.8
  410.6 1.7 fusion.190
  414.9 2.2 fusion.192
  417.0 9.6 fusion.188
  427.5 24.6 %fusion.189 = f32[512,16,4]{1,2,0:T(4,128)} fusion(f32[16,512,512]{2,1,0:T(8,128)} %fusion.188, s32[4,512]{0,1:T(8,128)S(1)} %bitcast.130), kind=kOutput, calls=%fused_computation.16.clone.1 | convolution fusion | flops 202375168 | bytes 16916480 | tf_op jit(solution)/shard_map/while/body/eval_jaxpr/tpb,hpb->htp/dot_general | solution.py:98
  453.7 1.6 iota_compare_fusion.8
  455.4 1.7 fusion.190
  459.7 2.2 fusion.192
  461.8 9.6 fusion.188
  472.3 24.6 %fusion.189 = f32[512,16,4]{1,2,0:T(4,128)} fusion(f32[16,512,512]{2,1,0:T(8,128)} %fusion.188, s32[4,512]{0,1:T(8,128)S(1)} %bitcast.130), kind=kOutput, calls=%fused_computation.16.clone.1 | convolution fusion | flops 202375168 | bytes 16916480 | tf_op jit(solution)/shard_map/while/body/eval_jaxpr/tpb,hpb->htp/dot_general | solution.py:98
  500.2 1.7 fusion.190
  504.4 2.1 fusion.192
  506.6 9.6 fusion.188
  517.1 24.6 %fusion.189 = f32[512,16,4]{1,2,0:T(4,128)} fusion(f32[16,512,512]{2,1,0:T(8,128)} %fusion.188, s32[4,512]{0,1:T(8,128)S(1)} %bitcast.130), kind=kOutput, calls=%fused_computation.16.clone.1 | convolution fusion | flops 202375168 | bytes 16916480 | tf_op jit(solution)/shard_map/while/body/eval_jaxpr/tpb,hpb->htp/dot_general | solution.py:98
  545.0 1.7 fusion.190
  549.2 2.2 fusion.192
  551.4 9.6 fusion.188
  561.9 24.6 %fusion.189 = f32[512,16,4]{1,2,0:T(4,128)} fusion(f32[16,512,512]{2,1,0:T(8,128)} %fusion.188, s32[4,512]{0,1:T(8,128)S(1)} %bitcast.130), kind=kOutput, calls=%fused_computation.16.clone.1 | convolution fusion | flops 202375168 | bytes 16916480 | tf_op jit(solution)/shard_map/while/body/eval_jaxpr/tpb,hpb->htp/dot_general | solution.py:98
  588.0 1.6 iota_compare_fusion.8
  589.7 1.7 fusion.190
  594.0 2.1 fusion.192
  596.1 9.6 fusion.188
  606.6 24.6 %fusion.189 = f32[512,16,4]{1,2,0:T(4,128)} fusion(f32[16,512,512]{2,1,0:T(8,128)} %fusion.188, s32[4,512]{0,1:T(8,128)S(1)} %bitcast.130), kind=kOutput, calls=%fused_computation.16.clone.1 | convolution fusion | flops 202375168 | bytes 16916480 | tf_op jit(solution)/shard_map/while/body/eval_jaxpr/tpb,hpb->htp/dot_general | solution.py:98
  634.5 1.7 fusion.190
  638.8 2.2 fusion.192
  640.9 9.6 fusion.188
  651.4 24.6 %fusion.189 = f32[512,16,4]{1,2,0:T(4,128)} fusion(f32[16,512,512]{2,1,0:T(8,128)} %fusion.188, s32[4,512]{0,1:T(8,128)S(1)} %bitcast.130), kind=kOutput, calls=%fused_computation.16.clone.1 | convolution fusion | flops 202375168 | bytes 16916480 | tf_op jit(solution)/shard_map/while/body/eval_jaxpr/tpb,hpb->htp/dot_general | solution.py:98
  679.3 1.7 fusion.190
  683.5 2.2 fusion.192
  685.7 9.6 fusion.188
  696.2 24.6 %fusion.189 = f32[512,16,4]{1,2,0:T(4,128)} fusion(f32[16,512,512]{2,1,0:T(8,128)} %fusion.188, s32[4,512]{0,1:T(8,128)S(1)} %bitcast.130), kind=kOutput, calls=%fused_computation.16.clone.1 | convolution fusion | flops 202375168 | bytes 16916480 | tf_op jit(solution)/shard_map/while/body/eval_jaxpr/tpb,hpb->htp/dot_general | solution.py:98
  724.1 1.7 fusion.190
  728.3 2.2 fusion.192
  731.9 74.3 %pmax.7 = f32[8,16,4]{2,1,0:T(8,128)S(1)} all-reduce(f32[8,16,4]{2,1,0:T(8,128)S(1)} %reduce_max.18), channel_id=1, replica_groups=mesh['req'=8,'seq'=16] {'seq'}, use_global_device_ids=true, to_apply=%region_8.9 | all-reduce | flops 512 | bytes 4096 | tf_op jit(solution)/shard_map/pmax | solution.py:130
  808.4 28.4 %while.23 = (s32[]{:T(128)}, f32[8,4,16,64]{3,1,2,0:T(4,128)}, f32[8,16,4]{1,2,0:T(4,128)S(1)}, bf16[8,512,16,64]{1,3,2,0:T(8,128)(2,1)}, f32[8,16,4,512]{3,2,1,0:T(4,128)}, /*index=5*/f32[8,16,4]{1,2,0:T(4,128)S(1)}, s32[]{:T(128)}) while((s32[]{:T(128)}, f32[8,4,16,64]{3,1,2,0:T(4,128)}, f32[8,16,4]{1,2,0:T(4,128)S(1)}, ...), condition=%wide.region_12.13_spmd, body=%wide.region_10.12_spmd.sunk | while | flops 4325314 | bytes 1351513 | solution.py:146
  809.7 2.3 fusion.180
  813.2 2.3 fusion.180
  816.8 2.3 fusion.180
  820.3 2.3 fusion.180
  823.9 2.3 fusion.180
  827.4 2.3 fusion.180
  831.0 2.3 fusion.180
  834.5 2.3 fusion.180
  836.9 69.6 %psum.22 = f32[8,16,4]{2,1,0:T(8,128)S(1)} all-reduce(f32[8,16,4]{2,1,0:T(8,128)S(1)} %copy.129), channel_id=1, replica_groups=mesh['req'=8,'seq'=16] {'seq'}, use_global_device_ids=true, to_apply=%region_14.15 | all-reduce | flops 512 | bytes 4096 | tf_op jit(solution)/shard_map/psum | solution.py:147
  907.0 77.9 %all-reduce.3.cloned.1.call-done = f32[8,4,16,64]{3,1,2,0:T(4,128)} async-done(((f32[8,4,16,64]{3,1,2,0:T(4,128)}), f32[8,4,16,64]{3,1,2,0:T(4,128)}) %all-reduce.3.cloned.1.call-update) | async-done | bytes 131088 | tf_op jit(solution)/shard_map/psum | solution.py:147
  988.2 2.3 convolution_convert_fusion.1
  990.5 80.3 %all-reduce.5.cloned.1.call-done = bf16[32,1024]{1,0:T(8,128)(2,1)} async-done(((bf16[32,1024]{1,0:T(8,128)(2,1)}), bf16[32,1024]{1,0:T(8,128)(2,1)}) %all-reduce.5.cloned.1.call-update) | async-done | bytes 65552 | tf_op jit(solution)/shard_map/psum | solution.py:166
  (249 shorter events, 84.4 us)
Async XLA Ops:
  6.5 979.9 %copy-start = (bf16[1024,1024]{1,0:T(8,128)(2,1)S(1)}, bf16[1024,1024]{1,0:T(8,128)(2,1)}, u32[]{:S(2)}) copy-start(bf16[1024,1024]{1,0:T(8,128)(2,1)} %param.25) | copy-start | bytes 6291460
  6.5 290.5 %all-gather.3.cloned.1.call-start = ((), (), s32[]{:S(2)}) async-start(), calls=%async_computation.2 | async-start | bytes 135266304 | tf_op jit(solution)/shard_map/all_gather | solution.py:58
  7.6 3.5 copy-start.1
  11.0 0.8 copy-start.16
  11.0 1.4 copy-start.17
  11.0 973.9 %all-reduce.3.cloned.1.call-start = ((), (), s32[]{:S(2)}) async-start(), calls=%async_computation | async-start | bytes 524288 | tf_op jit(solution)/shard_map/psum | solution.py:147
  12.4 325.6 %copy-start.8 = (f32[1,1024]{1,0:T(1,128)}, f32[1,1024]{1,0:T(1,128)S(1)}, u32[]{:S(2)}) copy-start(f32[1,1024]{1,0:T(1,128)S(1)} %get-tuple-element.215) | copy-start | bytes 12292
  13.0 325.0 %copy-start.10 = (f32[1,1024]{1,0:T(1,128)}, f32[1,1024]{1,0:T(1,128)S(1)}, u32[]{:S(2)}) copy-start(f32[1,1024]{1,0:T(1,128)S(1)} %get-tuple-element.219) | copy-start | bytes 12292
  16.9 2.3 copy-start.4
  19.2 0.6 copy-start.12
  19.2 0.6 copy-start.5
  337.6 4.9 copy-start.2
  337.8 0.7 copy-start.18
  338.0 0.5 copy-start.20
  372.3 436.1 %copy-start.15 = (f32[8,16,4]{1,2,0:T(4,128)S(1)}, f32[8,16,4]{1,2,0:T(4,128)}, u32[]{:S(2)}) copy-start(f32[8,16,4]{1,2,0:T(4,128)} %custom-call.5) | copy-start | bytes 6148
  408.9 3.5 copy-start.24
  408.9 4.1 copy-start.23
  453.6 3.5 copy-start.24
  453.7 4.1 copy-start.23
  498.4 3.5 copy-start.24
  498.4 4.1 copy-start.23
  543.2 3.5 copy-start.24
  543.2 4.1 copy-start.23
  588.0 3.5 copy-start.24
  588.0 4.1 copy-start.23
  632.7 3.5 copy-start.24
  632.7 4.1 copy-start.23
  677.5 3.5 copy-start.24
  677.5 4.1 copy-start.23
  722.3 3.5 copy-start.24
  722.3 4.1 copy-start.23
  808.3 98.5 %copy-start.3 = (bf16[32,1024]{1,0:T(8,128)(2,1)S(1)}, bf16[32,1024]{1,0:T(8,128)(2,1)}, u32[]{:S(2)}) copy-start(bf16[32,1024]{1,0:T(8,128)(2,1)} %get-tuple-element.208) | copy-start | bytes 196612
  836.8 149.6 %copy-start.9 = (f32[1,1024]{1,0:T(1,128)S(1)}, f32[1,1024]{1,0:T(1,128)}, u32[]{:S(2)}) copy-start(f32[1,1024]{1,0:T(1,128)} %copy-done.8) | copy-start | bytes 12292
  836.8 149.6 %copy-start.11 = (f32[1,1024]{1,0:T(1,128)S(1)}, f32[1,1024]{1,0:T(1,128)}, u32[]{:S(2)}) copy-start(f32[1,1024]{1,0:T(1,128)} %copy-done.10) | copy-start | bytes 12292
  836.8 149.6 %copy-start.19 = (f32[32]{0:T(128)S(1)}, f32[32]{0:T(128)}, u32[]{:S(2)}) copy-start(f32[32]{0:T(128)} %copy-done.18) | copy-start | bytes 388
  836.8 149.6 %copy-start.21 = (f32[32]{0:T(128)S(1)}, f32[32]{0:T(128)}, u32[]{:S(2)}) copy-start(f32[32]{0:T(128)} %copy-done.20) | copy-start | bytes 388
  906.8 164.0 %all-reduce.5.cloned.1.call-start = ((), (), s32[]{:S(2)}) async-start(), calls=%async_computation.1 | async-start | bytes 131072 | tf_op jit(solution)/shard_map/psum | solution.py:166
  986.2 2.0 copy-start.6
  986.2 2.0 copy-start.7
  986.2 2.0 copy-start.22
  986.4 86.5 %copy-start.13 = (f32[1,1024]{1,0:T(1,128)S(1)}, f32[1,1024]{1,0:T(1,128)}, u32[]{:S(2)}) copy-start(f32[1,1024]{1,0:T(1,128)} %get-tuple-element.213) | copy-start | bytes 12292
  986.4 86.5 %copy-start.14 = (f32[1,1024]{1,0:T(1,128)S(1)}, f32[1,1024]{1,0:T(1,128)}, u32[]{:S(2)}) copy-start(f32[1,1024]{1,0:T(1,128)} %get-tuple-element.217) | copy-start | bytes 12292
Sparse Core Ops, SparseCore 0:
  11.1 285.8 all-gather.2
  906.9 77.9 all-reduce.2
  990.6 80.1 all-reduce.4
